TPU v7x, 32 devices: a whole 2x2x4 slice. The times are simulated.
32 devices in a mesh: row: 8 (over z, y), col: 4 (over x, core).
Axes of the slice: x: 2, y: 2, z: 4, core: 2. Of those that a mesh axis runs over, the one named last changes fastest.
Arguments:
- tile_basis: bfloat16 [8, 4, 2304, 256], P('row', 'col'), may hold values from -6 to 6
- tile_coeffs: bfloat16 [8, 4, 2304, 256], P('row', 'col'), may hold values from -0.375 to 0.375
- panel_basis: bfloat16 [8, 256, 2304], P('row', 'col'), may hold values from -6 to 6
- panel_coeffs: bfloat16 [8, 256, 2304], P('row', 'col'), may hold values from -0.125 to 0.125
- tile_rank: int32 [8, 4], P('row', 'col'), may hold values from 64 to 256
- target_rank: int32 [8, 4], P('row', 'col'), may hold values from 64 to 256, as said below
- panel_rank: int32 [8], replicated, may hold values from 64 to 256
- owner_row: int32 [4], replicated, may hold values from 0 to 7, as said below
Outputs:
- fresh_basis: bfloat16 [8, 4, 2304, 256], P('row', 'col')
- fresh_coeffs: bfloat16 [8, 4, 2304, 256], P('row', 'col')
Inputs may be any that keep to these rules, and one draw needn't show every extreme that they name: `target_rank`: a tile's rank after recompression never exceeds its rank before. `owner_row`: distinct panel tile rows.
All inputs are finite; a program needn't handle non-finite values.
Results may differ from a plain program's by a relative error of at most 0.0068.
Values may be sent and summed in bfloat16 or wider, within the bound.
No kernel may reach another device: no remote copies, remote signals or barrier semaphores. Data moves between devices by JAX's collectives and lax.ppermute only.
A program may use at most 64 MiB of HBM per device.

v0:
```python
import math
import jax
import jax.numpy as jnp
from jax import lax
from jax.sharding import PartitionSpec as P

NB = 2304


def spread(value, axis, source):
    kept = jnp.where(lax.axis_index(axis) == source, value, 0).astype(value.dtype)
    return lax.psum(kept, axis)


def keep_columns(matrix, limit):
    flags = (jnp.arange(matrix.shape[1]) < limit).astype(matrix.dtype)
    return matrix * flags[None, :]


def keep_rows(matrix, limit):
    flags = (jnp.arange(matrix.shape[0]) < limit).astype(matrix.dtype)
    return matrix * flags[:, None]


def lead_product(first, second):
    return lax.dot_general(
        first, second, (((0,), (0,)), ((), ())), preferred_element_type=jnp.float32
    )


def tail_product(first, second):
    return lax.dot_general(
        first, second, (((1,), (1,)), ((), ())), preferred_element_type=jnp.float32
    )


def body(
    tile_basis,
    tile_coeffs,
    panel_basis,
    panel_coeffs,
    tile_rank,
    target_rank,
    panel_rank,
    owner_row,
):
    row_basis, row_coeffs = (
        lax.all_gather(panel_basis, "col", axis=1, tiled=True),
        lax.all_gather(panel_coeffs, "col", axis=1, tiled=True),
    )
    source = owner_row[lax.axis_index("col")]
    col_basis, col_coeffs = (spread(row_basis, "row", source), spread(row_coeffs, "row", source))
    here_rank = panel_rank[lax.axis_index("row")]
    there_rank = panel_rank[source]
    left_u = keep_rows(row_basis[0], here_rank)
    left_v = keep_rows(row_coeffs[0], here_rank)
    other_u = keep_rows(col_basis[0], there_rank)
    other_v = keep_rows(col_coeffs[0], there_rank)
    old_rank = tile_rank[0, 0]
    goal_rank = target_rank[0, 0]
    basis = keep_columns(tile_basis[0, 0], old_rank)
    coeffs = keep_columns(tile_coeffs[0, 0], old_rank)
    coupling = tail_product(left_v, other_v).astype(jnp.bfloat16)
    shifted = lead_product(left_u, coupling).astype(jnp.bfloat16)
    sketch = keep_columns(coeffs, goal_rank)
    core_upper = lead_product(coeffs, sketch).astype(jnp.bfloat16)
    core_lower = jnp.dot(other_u, sketch, preferred_element_type=jnp.float32).astype(jnp.bfloat16)
    sampled = jnp.dot(basis, core_upper, preferred_element_type=jnp.float32) - jnp.dot(
        shifted, core_lower, preferred_element_type=jnp.float32
    )
    extra = (jnp.arange(sampled.shape[1]) >= goal_rank).astype(jnp.float32)
    gram_matrix = lax.dot_general(
        sampled,
        sampled,
        (((0,), (0,)), ((), ())),
        precision=lax.Precision.HIGHEST,
        preferred_element_type=jnp.float32,
    )
    gram_matrix = gram_matrix + jnp.diag(extra)
    factor = jnp.linalg.cholesky(gram_matrix)
    orthonormal = jax.scipy.linalg.solve_triangular(factor, sampled.T, lower=True).T
    scaling = math.sqrt(NB)
    fresh_basis = (orthonormal * scaling).astype(jnp.bfloat16)
    reduced_upper = (lead_product(basis, fresh_basis) / scaling).astype(jnp.bfloat16)
    reduced_lower = (-lead_product(shifted, fresh_basis) / scaling).astype(jnp.bfloat16)
    fresh_coeffs = jnp.dot(
        coeffs, reduced_upper, preferred_element_type=jnp.float32
    ) + lead_product(other_u, reduced_lower)
    return (fresh_basis[None, None], fresh_coeffs.astype(jnp.bfloat16)[None, None])


def solution(mesh):
    return jax.shard_map(
        body,
        mesh=mesh,
        in_specs=(
            P("row", "col", None, None),
            P("row", "col", None, None),
            P("row", "col", None),
            P("row", "col", None),
            P("row", "col"),
            P("row", "col"),
            P(),
            P(),
        ),
        out_specs=(P("row", "col", None, None), P("row", "col", None, None)),
        check_vma=False,
    )
```

profile of v0, /device:TPU:0, one launch (start us, length us, event | category | flops | bytes accessed | tf_op | source)
XLA Modules:
  0.0 263.1 jit_solution(7175004458664713414)
XLA Ops:
  7.2 0.0 all-gather.3.cloned.1.call-start
  7.2 0.7 all-gather.3.cloned.1.call-update
  7.9 0.0 all-gather.5.cloned.1.call-start
  7.9 0.7 all-gather.5.cloned.1.call-update
  8.6 0.0 all-reduce.4.cloned.1.call-start
  8.7 1.3 dynamic_slice.10
  10.6 19.1 %all-gather.3.cloned.1.call-done = bf16[1,256,2304]{2,1,0:T(8,128)(2,1)} async-done(((bf16[1,64,2304]{2,1,0:T(8,128)(2,1)}), bf16[1,256,2304]{2,1,0:T(8,128)(2,1)}) %all-gather.3.cloned.1.call-update) | async-done | bytes 1179664 | tf_op jit(solution)/shard_map/all_gather | solution.py:48
  29.7 1.1 broadcast_select_fusion
  30.8 18.0 %all-gather.5.cloned.1.call-done = bf16[1,256,2304]{2,1,0:T(8,128)(2,1)} async-done(((bf16[1,64,2304]{2,1,0:T(8,128)(2,1)}), bf16[1,256,2304]{2,1,0:T(8,128)(2,1)}) %all-gather.5.cloned.1.call-update) | async-done | bytes 1179664 | tf_op jit(solution)/shard_map/all_gather | solution.py:49
  48.8 1.1 broadcast_select_fusion.1
  49.9 0.0 copy-start.8
  49.9 0.0 copy-start.2
  49.9 0.0 copy-start.6
  49.9 0.0 all-reduce.4.cloned.1.call-update
  53.3 0.0 copy-done.8
  53.3 0.6 fusion.93
  53.9 0.6 iota_multiply_fusion
  54.5 1.7 compare_convert_fusion.1
  56.2 0.0 copy-done.2
  56.2 0.0 copy-done.6
  56.2 0.0 copy-start.5
  56.2 2.9 %fusion.38 = f32[2304,256]{1,0:T(8,128)} fusion(bf16[1,1,2304,256]{3,2,1,0:T(8,128)(2,1)S(1)} %copy-done.6, bf16[1,1,2304,256]{3,2,1,0:T(8,128)(2,1)S(1)} %copy-done.2, bf16[256]{0:T(256)(128)(2,1)S(1)} %get-tuple-element.32, bf16[256]{0:T(256)(128)(2,1)S(1)} %get-tuple-element.33), kind=kOutput, calls=%fused_computation.39 | convolution fusion | flops 606404608 | bytes 4719616 | tf_op jit(solution)/shard_map/dot_general | solution.py:68
  59.1 102.9 %all-reduce.4.cloned.1.call-done = (bf16[1,256,2304]{2,1,0:T(8,128)(2,1)}, bf16[1,256,2304]{2,1,0:T(8,128)(2,1)}) async-done(((bf16[1,256,2304]{2,1,0:T(8,128)(2,1)}, bf16[1,256,2304]{2,1,0:T(8,128)(2,1)}), (bf16[1,256,2304]{2,1,0:T(8,128)(2,1)}, bf16[1,256,2304]{2,1,0:T(8,128)(2,1)})) %all-reduce.4.cloned.1.call-update) | async-done | bytes 2359312 | tf_op jit(solution)/shard_map/psum | solution.py:12
  162.1 0.0 copy-done.5
  162.1 0.0 copy-start
  162.1 4.3 %convolution_convert_fusion = bf16[2304,256]{1,0:T(8,128)(2,1)} fusion(bf16[1,256,2304]{2,1,0:T(8,128)(2,1)S(1)} %copy-done.5, bf16[1,256,2304]{2,1,0:T(8,128)(2,1)} %get-tuple-element.20, bf16[1,256,2304]{2,1,0:T(8,128)(2,1)} %all-gather.5.cloned.1.call-done, bf16[256]{0:T(256)(128)(2,1)S(1)} %get-tuple-element.34, bf16[256]{0:T(256)(128)(2,1)} %get-tuple-element.35), kind=kOutput, calls=%fused_computation.5 | convolution fusion | flops 606404608 | bytes 4719616 | tf_op jit(solution)/shard_map/dot_general | solution.py:26
  166.4 0.0 copy-done
  166.4 3.9 %convolution_subtract_fusion = f32[2304,256]{1,0:T(8,128)S(1)} fusion(f32[2304,256]{1,0:T(8,128)} %fusion.38, bf16[2304,256]{1,0:T(8,128)(2,1)} %convolution_convert_fusion, bf16[1,256,2304]{2,1,0:T(8,128)(2,1)S(1)} %copy-done, bf16[1,1,2304,256]{3,2,1,0:T(8,128)(2,1)} %param.9, bf16[256]{0:T(256)(128)(2,1)S(1)} %get-tuple-element.34, ...), kind=kOutput, calls=%fused_computation.3 | convolution fusion | flops 606404608 | bytes 8259072 | tf_op jit(solution)/shard_map/dot_general | solution.py:68
  170.4 3.9 %fusion.94 = f32[256,256]{1,0:T(8,128)S(1)} fusion(f32[2304,256]{1,0:T(8,128)S(1)} %convolution_subtract_fusion), kind=kOutput, calls=%fused_computation.92 | convolution fusion | flops 1811939328 | bytes 2621440 | tf_op jit(solution)/shard_map/dot_general | solution.py:72
  174.3 0.1 copy.10
  174.4 0.0 copy-start.9
  174.4 0.1 fusion.77
  174.5 11.7 %cholesky.49 = f32[128,128]{1,0:T(8,128)S(1)} custom-call(f32[128,128]{1,0:T(8,128)S(1)} %cholesky.115), custom_call_target="Cholesky" | custom-call | tf_op jit(solution)/shard_map/jit(cholesky)/cholesky | solution.py:80
  186.3 9.9 %custom-call.15 = f32[1,128,128]{1,2,0:T(8,128)S(1)} custom-call(f32[1,128,128]{2,1,0:T(8,128)S(1)} %get-tuple-element.27), custom_call_target="InvertDiagBlocksLowerTriangular" | custom-call | tf_op jit(solution)/shard_map/jit(cholesky)/cholesky | solution.py:80
  196.2 0.2 constant_dynamic-update-slice_fusion.1
  196.4 0.3 convolution_subtract_fusion.2
  196.7 11.7 %cholesky.103 = f32[128,128]{1,0:T(8,128)S(1)} custom-call(f32[128,128]{1,0:T(8,128)S(1)} %convolution_subtract_fusion.2), custom_call_target="Cholesky" | custom-call | tf_op jit(solution)/shard_map/jit(cholesky)/cholesky | solution.py:80
  208.4 0.7 compare_reduce_fusion
  209.1 0.6 compare_reduce_fusion.1
  211.1 0.0 copy-done.9
  211.1 0.1 triangular_solve.63
  211.1 5.2 %while.1 = (s32[]{:T(128)}, f32[256,256]{1,0:T(8,128)S(1)}, s32[2,2]{1,0:T(2,128)S(1)}, f32[2,128,128]{2,1,0:T(8,128)}, s32[]{:T(128)}) while((s32[]{:T(128)}, f32[256,256]{1,0:T(8,128)S(1)}, s32[2,2]{1,0:T(2,128)S(1)}, f32[2,128,128]{2,1,0:T(8,128)}, s32[]{:T(128)}) %tuple.30), condition=%wide.while_cond, body=%wide.while_body.sunk | while | flops 2 | bytes 132705 | solution.py:81
  211.1 0.6 fusion.104
  211.7 2.0 bitcast_dynamic-update-slice_fusion.2
  213.7 0.6 fusion.104
  214.3 2.0 bitcast_dynamic-update-slice_fusion.2
  216.3 0.0 copy-start.4
  216.3 21.2 %custom-call.16 = f32[2,128,128]{1,2,0:T(8,128)} custom-call(f32[2,128,128]{2,1,0:T(8,128)} %get-tuple-element.9), custom_call_target="InvertDiagBlocksLowerTriangular" | custom-call | tf_op jit(solution)/shard_map/jit(_solve_triangular)/triangular_solve | solution.py:81
  237.5 0.0 copy-done.4
  237.5 2.0 fusion.3
  239.5 0.0 copy-start.7
  239.5 2.9 %convolution_subtract_fusion.1 = f32[128,2304]{0,1:T(8,128)S(1)} fusion(f32[128,2304]{1,0:T(8,128)S(1)} %fusion.3, f32[256,2304]{0,1:T(8,128)S(1)} %bitcast.108, f32[256,256]{1,0:T(8,128)} %copy-done.4), kind=kOutput, calls=%fused_computation.6 | convolution fusion | flops 453279744 | bytes 3604480 | tf_op jit(solution)/shard_map/jit(_solve_triangular)/triangular_solve | solution.py:81
  242.4 0.0 copy-done.7
  242.4 0.0 copy-start.3
  242.4 1.2 fusion.81
  243.6 0.1 copy-done.3
  243.7 4.2 %fusion.5 = f32[2304,256]{1,0:T(8,128)} fusion(bf16[1,1,2304,256]{3,2,1,0:T(8,128)(2,1)S(1)} %copy-done.3, bf16[1,1,2304,256]{3,2,1,0:T(8,128)(2,1)} %param.8, bf16[256]{0:T(256)(128)(2,1)S(1)} %get-tuple-element.33, f32[128,2304]{1,0:T(8,128)S(1)} %fusion.81, f32[128,2304]{1,0:T(8,128)S(1)} %fusion.3), kind=kOutput, calls=%fused_computation.14 | convolution fusion | flops 607059968 | bytes 7078400 | tf_op jit(solution)/shard_map/dot_general | solution.py:86
  247.9 0.0 copy-start.1
  247.9 1.2 fusion.91
  249.1 0.5 copy-done.1
  249.6 4.6 %fusion.1 = bf16[1,1,2304,256]{3,2,1,0:T(8,128)(2,1)} fusion(f32[2304,256]{1,0:T(8,128)} %fusion.5, bf16[1,256,2304]{2,1,0:T(8,128)(2,1)S(1)} %copy-done.1, bf16[2304,256]{1,0:T(8,128)(2,1)} %convolution_convert_fusion, bf16[256]{0:T(256)(128)(2,1)S(1)} %get-tuple-element.34, f32[128,2304]{1,0:T(8,128)S(1)} %fusion.81, f32[128,2304]{1,0:T(8,128)S(1)} %fusion.3), kind=kOutput, calls=%fused_computation.7 | convolution fusion | flops 607715328 | bytes 8258048 | tf_op jit(solution)/shard_map/dot_general | solution.py:26
  254.2 2.4 copy.11
  (10 shorter events, 0.1 us)
Async XLA Ops:
  7.2 22.6 %all-gather.3.cloned.1.call-start = ((), (), s32[]{:S(2)}) async-start(), calls=%async_computation | async-start | bytes 1474560 | tf_op jit(solution)/shard_map/all_gather | solution.py:48
  7.9 40.9 %all-gather.5.cloned.1.call-start = ((), (), s32[]{:S(2)}) async-start(), calls=%async_computation.1 | async-start | bytes 1474560 | tf_op jit(solution)/shard_map/all_gather | solution.py:49
  8.6 153.4 %all-reduce.4.cloned.1.call-start = ((), (), s32[]{:S(2)}) async-start(), calls=%async_computation.2 | async-start | bytes 4718592 | tf_op jit(solution)/shard_map/psum | solution.py:12
  49.9 3.4 %copy-start.8 = (s32[8]{0:T(128)S(1)}, s32[8]{0:T(128)}, u32[]{:S(2)}) copy-start(s32[8]{0:T(128)} %param.14) | copy-start | bytes 100
  49.9 6.3 %copy-start.2 = (bf16[1,1,2304,256]{3,2,1,0:T(8,128)(2,1)S(1)}, bf16[1,1,2304,256]{3,2,1,0:T(8,128)(2,1)}, u32[]{:S(2)}) copy-start(bf16[1,1,2304,256]{3,2,1,0:T(8,128)(2,1)} %param.9) | copy-start | bytes 3538948
  49.9 6.3 %copy-start.6 = (bf16[1,1,2304,256]{3,2,1,0:T(8,128)(2,1)S(1)}, bf16[1,1,2304,256]{3,2,1,0:T(8,128)(2,1)}, u32[]{:S(2)}) copy-start(bf16[1,1,2304,256]{3,2,1,0:T(8,128)(2,1)} %param.8) | copy-start | bytes 3538948
  56.2 105.9 %copy-start.5 = (bf16[1,256,2304]{2,1,0:T(8,128)(2,1)S(1)}, bf16[1,256,2304]{2,1,0:T(8,128)(2,1)}, u32[]{:S(2)}) copy-start(bf16[1,256,2304]{2,1,0:T(8,128)(2,1)} %all-gather.3.cloned.1.call-done) | copy-start | bytes 3538948
  162.1 4.3 %copy-start = (bf16[1,256,2304]{2,1,0:T(8,128)(2,1)S(1)}, bf16[1,256,2304]{2,1,0:T(8,128)(2,1)}, u32[]{:S(2)}) copy-start(bf16[1,256,2304]{2,1,0:T(8,128)(2,1)} %get-tuple-element.21) | copy-start | bytes 3538948
  174.4 36.7 %copy-start.9 = (s32[2]{0:T(128)S(1)}, s32[2]{0:T(128)}, u32[]{:S(2)}) copy-start(s32[2]{0:T(128)} %iota_multiply_fusion) | copy-start | bytes 28
  216.3 21.2 %copy-start.4 = (f32[256,256]{1,0:T(8,128)}, f32[256,256]{1,0:T(8,128)S(1)}, u32[]{:S(2)}) copy-start(f32[256,256]{1,0:T(8,128)S(1)} %get-tuple-element.91) | copy-start | bytes 786436
  239.5 2.9 %copy-start.7 = (f32[2,128,128]{1,2,0:T(8,128)S(1)}, f32[2,128,128]{1,2,0:T(8,128)}, u32[]{:S(2)}) copy-start(f32[2,128,128]{1,2,0:T(8,128)} %custom-call.16) | copy-start | bytes 393220
  242.4 1.3 copy-start.3
  247.9 1.7 copy-start.1
Sparse Core Ops, SparseCore 0:
  9.6 20.1 all-gather.2
  31.3 17.4 all-gather.4
  53.0 109.0 all-reduce.3
where the time goes:
time: 264 us; the launch traced here: 263 us
  waiting for transfers between devices  141 us (53%)
  other arithmetic  61.6 us (23%)
  matrix products  30.4 us (12%)
  between operations  19.2 us (7%)
  local copies, waits for them, and re-layouts  10.3 us (4%)
    psum x1, waiting for transfers between devices, spread(): return lax.psum(kept, axis)  103 us
    another operation x7, other arithmetic, body(): factor = jnp.linalg.cholesky(gram_matrix)  34.7 us
    another operation x3, other arithmetic, body(): jax.scipy.linalg.solve_triangular(factor, sampled.T, lower=True)  21.8 us
    all_gather x1, waiting for transfers between devices, body(): lax.all_gather(panel_basis, 'col', axis=1, tiled=True)  19.1 us
    all_gather x1, waiting for transfers between devices, body(): lax.all_gather(panel_coeffs, 'col', axis=1, tiled=True)  18 us
    dot_general x2, matrix products, lead_product(): lax.dot_general(first, second, (((0,), (0,)), ((), ())), preferred_elemen...  8.91 us
    another operation x3, matrix products, body(): jax.scipy.linalg.solve_triangular(factor, sampled.T, lower=True)  6.08 us
  transfers between devices with their start and end apart: 3, of which 3 were waited for; matrix products, arithmetic and copies ran while one was open for 3% of the time, Pallas kernels for 0%

commit v1 on v0

--- a/solution.py
+++ b/solution.py
@@ -3,6 +3,7 @@
 import jax.numpy as jnp
 from jax import lax
 from jax.sharding import PartitionSpec as P
+from jax.lax import axis_index, ppermute, psum
 
 NB = 2304
 
@@ -44,9 +45,26 @@
     panel_rank,
     owner_row,
 ):
+
+    def try_all_region(w_in):
+        peer_axis = "col"
+        slots = psum(1, peer_axis)
+        samples = [(d, (d + 1) % slots) for d in range(slots)]
+        buffers = [(d, (d - 1) % slots) for d in range(slots)]
+        frame_out, value_now = ([w_in], [w_in])
+        for _ in range(slots // 2):
+            frame_out.append(ppermute(frame_out[-1], peer_axis, samples))
+        for _ in range((slots - 1) // 2):
+            value_now.append(ppermute(value_now[-1], peer_axis, buffers))
+        return jnp.roll(
+            jnp.concatenate([*frame_out[::-1], *value_now[1:]], axis=1),
+            (axis_index(peer_axis) - slots // 2) * w_in.shape[1],
+            axis=1,
+        )
+
     row_basis, row_coeffs = (
         lax.all_gather(panel_basis, "col", axis=1, tiled=True),
-        lax.all_gather(panel_coeffs, "col", axis=1, tiled=True),
+        try_all_region(panel_coeffs),
     )
     source = owner_row[lax.axis_index("col")]
     col_basis, col_coeffs = (spread(row_basis, "row", source), spread(row_coeffs, "row", source))

time: 264 us -> 251 us (0.951)
  waiting for transfers between devices: 141 us -> 124 us
    all_gather x1 -> x0, waiting for transfers between devices: 18 us -> none  [body(): lax.all_gather(panel_coeffs, 'col', axis=1, tiled=True)]
    ppermute x0 -> x3, waiting for transfers between devices: none -> 11.9 us  [the longest x2 9.15 us: try_all_region(): frame_out.append(ppermute(frame_out[-1], peer_axis, samples))]
    all_gather x1, waiting for transfers between devices: 19.1 us -> 9.42 us  [body(): lax.all_gather(panel_basis, 'col', axis=1, tiled=True)]
  transfers between devices with their start and end apart: 3 -> 5, of which waited for: 3 -> 5; matrix products, arithmetic and copies ran while one was open for 3% -> 3% of each run, Pallas kernels for 0% -> 0%
where the time goes in v1:
time: 251 us; the launch traced here: 250 us
  waiting for transfers between devices  124 us (49%)
  other arithmetic  61.8 us (25%)
  matrix products  30.4 us (12%)
  between operations  19.7 us (8%)
  local copies, waits for them, and re-layouts  12 us (5%)
    psum x1, waiting for transfers between devices, spread(): return lax.psum(kept, axis)  103 us
    another operation x7, other arithmetic, body(): factor = jnp.linalg.cholesky(gram_matrix)  34.7 us
    another operation x3, other arithmetic, body(): jax.scipy.linalg.solve_triangular(factor, sampled.T, lower=True)  21.7 us
    all_gather x1, waiting for transfers between devices, body(): lax.all_gather(panel_basis, 'col', axis=1, tiled=True)  9.42 us
    ppermute x2, waiting for transfers between devices, try_all_region(): frame_out.append(ppermute(frame_out[-1], peer_axis, samples))  9.15 us
    dot_general x2, matrix products, lead_product(): lax.dot_general(first, second, (((0,), (0,)), ((), ())), preferred_elemen...  8.91 us
    another operation x3, matrix products, body(): jax.scipy.linalg.solve_triangular(factor, sampled.T, lower=True)  6.08 us
    another operation x6, local copies, waits for them, and re-layouts  5.17 us
  transfers between devices with their start and end apart: 5, of which 5 were waited for; matrix products, arithmetic and copies ran while one was open for 3% of the time, Pallas kernels for 0%

profile of v1, /device:TPU:0, one launch (start us, length us, event | category | flops | bytes accessed | tf_op | source)
XLA Modules:
  0.0 250.5 jit_solution(17720448582142560657)
XLA Ops:
  7.2 0.0 copy-start.6
  7.2 0.0 all-gather.2.cloned.1.call-start
  7.2 0.5 collective-permute-start
  7.7 6.5 %collective-permute-done = bf16[1,64,2304]{2,1,0:T(8,128)(2,1)S(1)} collective-permute-done((bf16[1,64,2304]{2,1,0:T(8,128)(2,1)}, bf16[1,64,2304]{2,1,0:T(8,128)(2,1)S(1)}, u32[]{:S(2)}, u32[]{:S(2)}) %collective-permute-start) | collective-permute-done | bytes 294944 | tf_op jit(solution)/shard_map/ppermute | solution.py:56
  14.3 0.0 collective-permute-start.1
  14.3 1.7 collective-permute-start.2
  16.0 0.0 all-gather.2.cloned.1.call-update
  16.0 0.0 all-reduce.4.cloned.1.call-start
  16.1 1.3 dynamic_slice.15
  18.1 2.6 %collective-permute-done.1 = bf16[1,64,2304]{2,1,0:T(8,128)(2,1)S(1)} collective-permute-done((bf16[1,64,2304]{2,1,0:T(8,128)(2,1)S(1)}, bf16[1,64,2304]{2,1,0:T(8,128)(2,1)S(1)}, u32[]{:S(2)}, u32[]{:S(2)}) %collective-permute-start.1) | collective-permute-done | bytes 294944 | tf_op jit(solution)/shard_map/ppermute | solution.py:56
  20.8 0.0 copy-done.6
  20.8 2.7 %collective-permute-done.2 = bf16[1,64,2304]{2,1,0:T(8,128)(2,1)S(1)} collective-permute-done((bf16[1,64,2304]{2,1,0:T(8,128)(2,1)}, bf16[1,64,2304]{2,1,0:T(8,128)(2,1)S(1)}, u32[]{:S(2)}, u32[]{:S(2)}) %collective-permute-start.2) | collective-permute-done | bytes 294944 | tf_op jit(solution)/shard_map/ppermute | solution.py:58
  23.6 0.0 copy-start.8
  23.7 1.4 copy-done.8
  25.1 1.2 broadcast_select_fusion.1
  26.3 9.4 %all-gather.2.cloned.1.call-done = bf16[1,256,2304]{2,1,0:T(8,128)(2,1)} async-done(((bf16[1,64,2304]{2,1,0:T(8,128)(2,1)}), bf16[1,256,2304]{2,1,0:T(8,128)(2,1)}) %all-gather.2.cloned.1.call-update) | async-done | bytes 1179664 | tf_op jit(solution)/shard_map/all_gather | solution.py:66
  35.7 1.1 broadcast_select_fusion
  36.8 0.0 copy-start.10
  36.8 0.0 all-reduce.4.cloned.1.call-update
  40.3 0.0 copy-done.10
  40.3 0.7 fusion.96
  41.0 0.5 iota_multiply_fusion
  41.5 1.8 compare_convert_fusion.1
  43.4 0.0 copy-done.2
  43.4 0.0 copy-done.7
  43.4 0.0 copy-start.5
  43.4 2.9 %fusion.38 = f32[2304,256]{1,0:T(8,128)} fusion(bf16[1,1,2304,256]{3,2,1,0:T(8,128)(2,1)S(1)} %copy-done.7, bf16[1,1,2304,256]{3,2,1,0:T(8,128)(2,1)S(1)} %copy-done.2, bf16[256]{0:T(256)(128)(2,1)S(1)} %get-tuple-element.32, bf16[256]{0:T(256)(128)(2,1)S(1)} %get-tuple-element.33), kind=kOutput, calls=%fused_computation.39 | convolution fusion | flops 606404608 | bytes 4719616 | tf_op jit(solution)/shard_map/dot_general | solution.py:86
  46.3 102.7 %all-reduce.4.cloned.1.call-done = (bf16[1,256,2304]{2,1,0:T(8,128)(2,1)}, bf16[1,256,2304]{2,1,0:T(8,128)(2,1)}) async-done(((bf16[1,256,2304]{2,1,0:T(8,128)(2,1)}, bf16[1,256,2304]{2,1,0:T(8,128)(2,1)}), (bf16[1,256,2304]{2,1,0:T(8,128)(2,1)}, bf16[1,256,2304]{2,1,0:T(8,128)(2,1)})) %all-reduce.4.cloned.1.call-update) | async-done | bytes 2359312 | tf_op jit(solution)/shard_map/psum | solution.py:13
  149.0 0.0 copy-done.5
  149.0 4.3 %convolution_convert_fusion = bf16[2304,256]{1,0:T(8,128)(2,1)} fusion(bf16[1,256,2304]{2,1,0:T(8,128)(2,1)S(1)} %copy-done.5, bf16[1,256,2304]{2,1,0:T(8,128)(2,1)} %get-tuple-element.20, bf16[1,512,2304]{2,1,0:T(8,128)(2,1)} %copy-done.8, s32[]{:T(128)S(6)} %select_n.48, bf16[256]{0:T(256)(128)(2,1)S(1)} %get-tuple-element.34, ...), kind=kOutput, calls=%fused_computation.5 | convolution fusion | flops 608174080 | bytes 4720132 | tf_op jit(solution)/shard_map/dot_general | solution.py:27
  153.3 0.0 copy-done
  153.3 3.9 %convolution_subtract_fusion = f32[2304,256]{1,0:T(8,128)S(1)} fusion(f32[2304,256]{1,0:T(8,128)} %fusion.38, bf16[2304,256]{1,0:T(8,128)(2,1)} %convolution_convert_fusion, bf16[1,256,2304]{2,1,0:T(8,128)(2,1)S(1)} %copy-done, bf16[1,1,2304,256]{3,2,1,0:T(8,128)(2,1)} %param.9, bf16[256]{0:T(256)(128)(2,1)S(1)} %get-tuple-element.34, ...), kind=kOutput, calls=%fused_computation.3 | convolution fusion | flops 606404608 | bytes 8259072 | tf_op jit(solution)/shard_map/dot_general | solution.py:86
  157.3 3.9 %fusion.97 = f32[256,256]{1,0:T(8,128)S(1)} fusion(f32[2304,256]{1,0:T(8,128)S(1)} %convolution_subtract_fusion), kind=kOutput, calls=%fused_computation.102 | convolution fusion | flops 1811939328 | bytes 2621440 | tf_op jit(solution)/shard_map/dot_general | solution.py:90
  161.2 0.1 copy.10
  161.3 0.0 copy-start.11
  161.3 0.1 fusion.78
  161.4 11.8 %cholesky.49 = f32[128,128]{1,0:T(8,128)S(1)} custom-call(f32[128,128]{1,0:T(8,128)S(1)} %cholesky.115), custom_call_target="Cholesky" | custom-call | tf_op jit(solution)/shard_map/jit(cholesky)/cholesky | solution.py:98
  173.3 9.8 %custom-call.15 = f32[1,128,128]{1,2,0:T(8,128)S(1)} custom-call(f32[1,128,128]{2,1,0:T(8,128)S(1)} %get-tuple-element.27), custom_call_target="InvertDiagBlocksLowerTriangular" | custom-call | tf_op jit(solution)/shard_map/jit(cholesky)/cholesky | solution.py:98
  183.1 0.2 constant_dynamic-update-slice_fusion.9
  183.3 0.3 convolution_subtract_fusion.2
  183.6 11.7 %cholesky.103 = f32[128,128]{1,0:T(8,128)S(1)} custom-call(f32[128,128]{1,0:T(8,128)S(1)} %convolution_subtract_fusion.2), custom_call_target="Cholesky" | custom-call | tf_op jit(solution)/shard_map/jit(cholesky)/cholesky | solution.py:98
  195.3 0.7 compare_reduce_fusion
  196.0 0.6 compare_reduce_fusion.1
  197.9 0.0 copy-done.11
  198.0 0.1 triangular_solve.63
  198.0 5.4 %while.1 = (s32[]{:T(128)}, f32[256,256]{1,0:T(8,128)S(1)}, s32[2,2]{1,0:T(2,128)S(1)}, f32[2,128,128]{2,1,0:T(8,128)}, s32[]{:T(128)}) while((s32[]{:T(128)}, f32[256,256]{1,0:T(8,128)S(1)}, s32[2,2]{1,0:T(2,128)S(1)}, f32[2,128,128]{2,1,0:T(8,128)}, s32[]{:T(128)}) %tuple.30), condition=%wide.while_cond, body=%wide.while_body.sunk | while | flops 2 | bytes 132705 | solution.py:99
  198.2 0.6 fusion.107
  198.8 2.0 bitcast_dynamic-update-slice_fusion.2
  200.8 0.6 fusion.107
  201.4 2.0 bitcast_dynamic-update-slice_fusion.2
  203.4 21.2 %custom-call.16 = f32[2,128,128]{1,2,0:T(8,128)} custom-call(f32[2,128,128]{2,1,0:T(8,128)} %get-tuple-element.9), custom_call_target="InvertDiagBlocksLowerTriangular" | custom-call | tf_op jit(solution)/shard_map/jit(_solve_triangular)/triangular_solve | solution.py:99
  224.5 0.0 copy-done.4
  224.6 2.0 fusion.3
  226.6 0.0 copy-start.9
  226.6 2.9 %convolution_subtract_fusion.1 = f32[128,2304]{0,1:T(8,128)S(1)} fusion(f32[128,2304]{1,0:T(8,128)S(1)} %fusion.3, f32[256,2304]{0,1:T(8,128)S(1)} %bitcast.108, f32[256,256]{1,0:T(8,128)} %copy-done.4), kind=kOutput, calls=%fused_computation.6 | convolution fusion | flops 453279744 | bytes 3604480 | tf_op jit(solution)/shard_map/jit(_solve_triangular)/triangular_solve | solution.py:99
  229.5 0.0 copy-done.9
  229.5 0.0 copy-start.3
  229.5 1.2 fusion.82
  230.7 0.1 copy-done.3
  230.8 4.2 %fusion.5 = f32[2304,256]{1,0:T(8,128)} fusion(bf16[1,1,2304,256]{3,2,1,0:T(8,128)(2,1)S(1)} %copy-done.3, bf16[1,1,2304,256]{3,2,1,0:T(8,128)(2,1)} %param.8, bf16[256]{0:T(256)(128)(2,1)S(1)} %get-tuple-element.33, f32[128,2304]{1,0:T(8,128)S(1)} %fusion.82, f32[128,2304]{1,0:T(8,128)S(1)} %fusion.3), kind=kOutput, calls=%fused_computation.14 | convolution fusion | flops 607059968 | bytes 7078400 | tf_op jit(solution)/shard_map/dot_general | solution.py:104
  235.0 1.2 fusion.94
  236.2 0.5 copy-done.1
  236.7 4.6 %fusion.1 = bf16[1,1,2304,256]{3,2,1,0:T(8,128)(2,1)} fusion(f32[2304,256]{1,0:T(8,128)} %fusion.5, bf16[1,256,2304]{2,1,0:T(8,128)(2,1)S(1)} %copy-done.1, bf16[2304,256]{1,0:T(8,128)(2,1)} %convolution_convert_fusion, bf16[256]{0:T(256)(128)(2,1)S(1)} %get-tuple-element.34, f32[128,2304]{1,0:T(8,128)S(1)} %fusion.82, f32[128,2304]{1,0:T(8,128)S(1)} %fusion.3), kind=kOutput, calls=%fused_computation.7 | convolution fusion | flops 607715328 | bytes 8258048 | tf_op jit(solution)/shard_map/dot_general | solution.py:27
  241.3 2.4 copy.11
  (23 shorter events, 0.3 us)
Async XLA Ops:
  7.2 13.6 %copy-start.6 = (bf16[1,64,2304]{2,1,0:T(8,128)(2,1)S(1)}, bf16[1,64,2304]{2,1,0:T(8,128)(2,1)}, u32[]{:S(2)}) copy-start(bf16[1,64,2304]{2,1,0:T(8,128)(2,1)} %param.11) | copy-start | bytes 884740
  7.2 28.5 %all-gather.2.cloned.1.call-start = ((), (), s32[]{:S(2)}) async-start(), calls=%async_computation | async-start | bytes 1474560 | tf_op jit(solution)/shard_map/all_gather | solution.py:66
  7.2 7.0 %collective-permute-start = (bf16[1,64,2304]{2,1,0:T(8,128)(2,1)}, bf16[1,64,2304]{2,1,0:T(8,128)(2,1)S(1)}, u32[]{:S(2)}, u32[]{:S(2)}) collective-permute-start(bf16[1,64,2304]{2,1,0:T(8,128)(2,1)} %param.11), channel_id=1, source_target_pairs={{0,1},{1,2},{2,3},{3,0},{4,5},{5,6},{6,7},{7,4},{8,9},{9,10},{10,1... | collective-permute-start | bytes 884744 | tf_op jit(solution)/shard_map/ppermute | solution.py:56
  14.3 6.4 %collective-permute-start.1 = (bf16[1,64,2304]{2,1,0:T(8,128)(2,1)S(1)}, bf16[1,64,2304]{2,1,0:T(8,128)(2,1)S(1)}, u32[]{:S(2)}, u32[]{:S(2)}) collective-permute-start(bf16[1,64,2304]{2,1,0:T(8,128)(2,1)S(1)} %collective-permute-done), channel_id=1, source_target_pairs={{0,1},{1,2},{2,3},{3,0},{4,5},{5,6},{6,7},{7,4},{8,9},{9,10},{10,1... | collective-permute-start | bytes 884744 | tf_op jit(solution)/shard_map/ppermute | solution.py:56
  14.3 9.2 %collective-permute-start.2 = (bf16[1,64,2304]{2,1,0:T(8,128)(2,1)}, bf16[1,64,2304]{2,1,0:T(8,128)(2,1)S(1)}, u32[]{:S(2)}, u32[]{:S(2)}) collective-permute-start(bf16[1,64,2304]{2,1,0:T(8,128)(2,1)} %param.11), channel_id=1, source_target_pairs={{0,3},{1,0},{2,1},{3,2},{4,7},{5,4},{6,5},{7,6},{8,11},{9,8},{10,9... | collective-permute-start | bytes 884744 | tf_op jit(solution)/shard_map/ppermute | solution.py:58
  16.0 133.0 %all-reduce.4.cloned.1.call-start = ((), (), s32[]{:S(2)}) async-start(), calls=%async_computation.1 | async-start | bytes 4718592 | tf_op jit(solution)/shard_map/psum | solution.py:13
  23.6 1.4 copy-start.8
  36.8 3.5 %copy-start.10 = (s32[8]{0:T(128)S(1)}, s32[8]{0:T(128)}, u32[]{:S(2)}) copy-start(s32[8]{0:T(128)} %param.14) | copy-start | bytes 100
  36.8 6.6 %copy-start.2 = (bf16[1,1,2304,256]{3,2,1,0:T(8,128)(2,1)S(1)}, bf16[1,1,2304,256]{3,2,1,0:T(8,128)(2,1)}, u32[]{:S(2)}) copy-start(bf16[1,1,2304,256]{3,2,1,0:T(8,128)(2,1)} %param.9) | copy-start | bytes 3538948
  36.8 6.6 %copy-start.7 = (bf16[1,1,2304,256]{3,2,1,0:T(8,128)(2,1)S(1)}, bf16[1,1,2304,256]{3,2,1,0:T(8,128)(2,1)}, u32[]{:S(2)}) copy-start(bf16[1,1,2304,256]{3,2,1,0:T(8,128)(2,1)} %param.8) | copy-start | bytes 3538948
  43.4 105.6 %copy-start.5 = (bf16[1,256,2304]{2,1,0:T(8,128)(2,1)S(1)}, bf16[1,256,2304]{2,1,0:T(8,128)(2,1)}, u32[]{:S(2)}) copy-start(bf16[1,256,2304]{2,1,0:T(8,128)(2,1)} %all-gather.2.cloned.1.call-done) | copy-start | bytes 3538948
  149.0 4.3 %copy-start = (bf16[1,256,2304]{2,1,0:T(8,128)(2,1)S(1)}, bf16[1,256,2304]{2,1,0:T(8,128)(2,1)}, u32[]{:S(2)}) copy-start(bf16[1,256,2304]{2,1,0:T(8,128)(2,1)} %get-tuple-element.21) | copy-start | bytes 3538948
  161.3 36.7 %copy-start.11 = (s32[2]{0:T(128)S(1)}, s32[2]{0:T(128)}, u32[]{:S(2)}) copy-start(s32[2]{0:T(128)} %iota_multiply_fusion) | copy-start | bytes 28
  203.4 21.2 %copy-start.4 = (f32[256,256]{1,0:T(8,128)}, f32[256,256]{1,0:T(8,128)S(1)}, u32[]{:S(2)}) copy-start(f32[256,256]{1,0:T(8,128)S(1)} %get-tuple-element.90) | copy-start | bytes 786436
  226.6 2.9 %copy-start.9 = (f32[2,128,128]{1,2,0:T(8,128)S(1)}, f32[2,128,128]{1,2,0:T(8,128)}, u32[]{:S(2)}) copy-start(f32[2,128,128]{1,2,0:T(8,128)} %custom-call.16) | copy-start | bytes 393220
  229.5 1.3 copy-start.3
  235.0 1.7 copy-start.1
Sparse Core Ops, SparseCore 0:
  16.2 19.5 all-gather.1
  39.9 109.0 all-reduce.3
